TPU v7x, 32 devices: a whole 2x2x4 slice. The times are simulated.
32 devices in a mesh: conv: 2 (over x), seq: 8 (over z, y), head: 2 (over core).
Axes of the slice: x: 2, y: 2, z: 4, core: 2. Of those that a mesh axis runs over, the one named last changes fastest.
Arguments:
- queries: bfloat16 [3072, 2048], P(('conv', 'seq'), 'head'), parts along dimension 0, may hold values from -10 to 10, as said below
- key_states: bfloat16 [3072, 512], P(('conv', 'seq'), 'head'), parts along dimension 0, may hold values from -5 to 5, as said below
- value_states: bfloat16 [3072, 512], P(('conv', 'seq'), 'head'), parts along dimension 0, may hold values from -16 to 16
- out_weight: bfloat16 [2048, 4096], P('head'), may hold values from -0.125 to 0.125
- turn_lengths: int32 [32], P('conv'), parts along dimension 0, may hold values from 1 to 959, as said below
- block_flags: int32 [16, 8], P(('conv', 'seq')), parts along dimension 0, may hold values 0 or 1
Outputs:
- pooled: float32 [32, 4096], P(('conv', 'seq'), 'head'), parts along dimension 0
There are 2 independent parts, one for each index of `conv`. A program takes and returns all parts, laid end to end along the dimension named above; an argument that names none is the same for every part. Nothing has to cross between parts.
Inputs may be any that keep to these rules, and one draw needn't show every extreme that they name: `queries`: every entry lies within the stated bounds. `key_states`: every entry lies within the stated bounds. `turn_lengths`: the lengths sum to 1536; turn 0 has one token and turn 1, the longest, has exactly 959 tokens.
All inputs are finite; a program needn't handle non-finite values. No bound on the sum of `block_flags` on one device may be relied on, other than what follows from the above.
Results may differ from a plain program's by a relative error of at most 0.0035.
Values may be sent and summed in bfloat16 or wider, within the bound.
A program may use at most 128 MiB of HBM per device.

v0:
```python
import math

import jax
import jax.numpy as jnp
from jax import lax
from jax.sharding import PartitionSpec as P

HD = 128


big_negative = -1e30
log_two_e = 1.4426950408889634


def on_device(queries, key_states, value_states, out_weight, turn_lengths, block_flags):
    q_rows = queries.shape[0]
    heads_here = queries.shape[1] // HD
    groups = key_states.shape[1] // HD
    repeat = heads_here // groups
    factor = log_two_e / math.sqrt(HD)
    my_index = lax.axis_index("seq")
    own_pos = my_index * q_rows + jnp.arange(q_rows, dtype=jnp.int32)
    block_count = block_flags.shape[1]
    row_pick = jnp.zeros((q_rows,), jnp.int32)
    query_block = own_pos // q_rows
    grouped = queries.reshape(q_rows, groups, repeat, HD)

    def mask_for(key_start, length):
        key_pos = key_start + jnp.arange(length, dtype=jnp.int32)
        key_block = key_pos // q_rows
        hits = key_block[:, None] == jnp.arange(block_count, dtype=jnp.int32)[None, :]
        allowed = jnp.sum(jnp.where(hits[None], block_flags[:, None, :], 0), axis=2)
        allowed_rows = jnp.where(row_pick[:, None] == 1, allowed[-1][None, :], allowed[0][None, :])
        causal = key_pos[None, :] <= own_pos[:, None]
        return causal & ((key_block[None, :] == query_block[:, None]) | (allowed_rows == 1))

    def attend(state, key_rows, value_rows, key_start):
        run_top, run_sum, totals = state
        length = key_rows.shape[0]
        visible = mask_for(key_start, length)[None, None]
        logit = (
            jnp.einsum(
                "qgrd,kgd->grqk",
                grouped,
                key_rows.reshape(length, groups, HD),
                preferred_element_type=jnp.float32,
            )
            * factor
        )
        logit = jnp.where(visible, logit, big_negative)
        new_top = jnp.maximum(run_top, jnp.ceil(jnp.max(logit, axis=-1)))
        weights = jnp.where(visible, jnp.exp2(logit - new_top[..., None]), 0.0)
        rescale = jnp.exp2(run_top - new_top)
        run_sum = run_sum * rescale + jnp.sum(weights, axis=-1)
        update = jnp.einsum(
            "grqk,kgd->grqd",
            weights.astype(jnp.bfloat16),
            value_rows.reshape(length, groups, HD),
            preferred_element_type=jnp.float32,
        )
        totals = totals * rescale[..., None] + update
        return (new_top, run_sum, totals)

    start_state = (
        jnp.full((groups, repeat, q_rows), big_negative, jnp.float32),
        jnp.zeros((groups, repeat, q_rows), jnp.float32),
        jnp.zeros((groups, repeat, q_rows, HD), jnp.float32),
    )
    key_piece = lax.all_gather(key_states, "seq", axis=0, tiled=True)
    value_piece = lax.all_gather(value_states, "seq", axis=0, tiled=True)
    length = key_piece.shape[0]
    width_step = math.gcd(length, 1024)

    def one_block(number, carried):
        offset = number * width_step
        key_rows = lax.dynamic_slice_in_dim(key_piece, offset, width_step, 0)
        value_rows = lax.dynamic_slice_in_dim(value_piece, offset, width_step, 0)
        return attend(carried, key_rows, value_rows, offset)

    run_top, run_sum, totals = lax.fori_loop(0, length // width_step, one_block, start_state)
    attended_work = (
        (totals / run_sum[..., None])
        .transpose(2, 0, 1, 3)
        .reshape(q_rows, heads_here * HD)
        .astype(jnp.bfloat16)
    )
    turn_ends = jnp.cumsum(turn_lengths)
    starts = turn_ends - turn_lengths
    member = (starts[:, None] <= own_pos[None, :]) & (own_pos[None, :] < turn_ends[:, None])
    turn_share = jnp.where(member, 1.0, 0.0).astype(jnp.float32) / turn_lengths[:, None].astype(
        jnp.float32
    )
    partial_rows = jnp.dot(attended_work, out_weight, preferred_element_type=jnp.float32)
    projected_rows = lax.psum_scatter(partial_rows, "head", scatter_dimension=1, tiled=True)
    pooled_part = jnp.dot(turn_share, projected_rows, precision=lax.Precision.HIGHEST)
    return lax.psum_scatter(pooled_part, "seq", scatter_dimension=0, tiled=True)


def solution(mesh):
    in_specs = (
        P(("conv", "seq"), "head"),
        P(("conv", "seq"), "head"),
        P(("conv", "seq"), "head"),
        P("head", None),
        P("conv"),
        P(("conv", "seq"), None),
    )
    out_specs = P(("conv", "seq"), "head")
    return jax.shard_map(
        on_device, mesh=mesh, in_specs=in_specs, out_specs=out_specs, check_vma=False
    )
```

profile of v0, /device:TPU:0, one launch (start us, length us, event | category | flops | bytes accessed | tf_op | source)
XLA Modules:
  0.0 211.3 jit_solution(6904133844643909026)
XLA Ops:
  6.5 36.3 %all_gather.6 = bf16[1536,256]{1,0:T(8,128)(2,1)} all-gather(bf16[192,256]{1,0:T(8,128)(2,1)} %param.9), channel_id=1, replica_groups=mesh['conv'=2,'seq'=8,'head'=2] {'seq'}, dimensions={0}, use_global_device_ids=true | all-gather | bytes 884736 | tf_op jit(solution)/shard_map/all_gather | solution.py:69
  42.9 34.2 %all_gather.7 = bf16[1536,256]{1,0:T(8,128)(2,1)} all-gather(bf16[192,256]{1,0:T(8,128)(2,1)} %param.10), channel_id=1, replica_groups=mesh['conv'=2,'seq'=8,'head'=2] {'seq'}, dimensions={0}, use_global_device_ids=true | all-gather | bytes 884736 | tf_op jit(solution)/shard_map/all_gather | solution.py:70
  77.1 1.3 reshape.229
  78.4 0.8 copy.26
  79.2 28.0 %while.22 = (s32[]{:T(128)}, f32[2,4,192]{2,1,0:T(4,128)S(1)}, f32[2,4,192]{2,1,0:T(4,128)S(1)}, f32[2,4,192,128]{3,2,1,0:T(8,128)}, s32[1,8]{1,0:T(1,128)S(1)},...) while((s32[]{:T(128)}, f32[2,4,192]{2,1,0:T(4,128)S(1)}, ...), condition=%wide.region_5.6_spmd.clone.clone.clone, body=%wide.region_1.5_spmd.clone.clone.clone.sunk | while | flops 415462080 | bytes 14534883 | solution.py:80
  79.5 1.1 constant_dynamic-slice_fusion.4
  80.6 0.8 copy.39
  81.4 1.8 fusion.54
  83.3 1.2 fusion.55
  84.5 0.8 copy.40
  85.3 3.1 %fusion.57 = f32[2,4,192,128]{3,2,1,0:T(8,128)} fusion(bf16[512,2,128,1]{0,2,3,1:T(8,128)(2,1)} %bitcast.53, f32[2,512,192,4]{1,2,3,0:T(8,128)S(1)} %get-tuple-element.465, f32[2,4,192]{2,1,0:T(4,128)S(1)} %ceil_maximum_fusion.2, pred[192,512]{1,0:T(8,128)(4,1)S(1)} %or_and_fusion.2, f32[2,4,192,128]{3,2,1,0:T(8,128)} %get-tuple-element.485, ...), kind=kOutput, calls=%fused_computation.9.clone.1 | convolution fusion | flops 206635008 | bytes 5091329 | tf_op jit(solution)/shard_map/while/body/eval_jaxpr/grqk,kgd->grqd/dot_general | solution.py:55
  88.8 1.1 constant_dynamic-slice_fusion.4
  89.8 0.8 copy.39
  90.7 1.8 fusion.54
  92.5 1.2 fusion.55
  93.8 0.8 copy.40
  94.6 3.2 %fusion.57 = f32[2,4,192,128]{3,2,1,0:T(8,128)} fusion(bf16[512,2,128,1]{0,2,3,1:T(8,128)(2,1)} %bitcast.53, f32[2,512,192,4]{1,2,3,0:T(8,128)S(1)} %get-tuple-element.465, f32[2,4,192]{2,1,0:T(4,128)S(1)} %ceil_maximum_fusion.2, pred[192,512]{1,0:T(8,128)(4,1)S(1)} %or_and_fusion.2, f32[2,4,192,128]{3,2,1,0:T(8,128)} %get-tuple-element.485, ...), kind=kOutput, calls=%fused_computation.9.clone.1 | convolution fusion | flops 206635008 | bytes 5091329 | tf_op jit(solution)/shard_map/while/body/eval_jaxpr/grqk,kgd->grqd/dot_general | solution.py:55
  98.1 1.1 constant_dynamic-slice_fusion.4
  99.2 0.8 copy.39
  100.1 1.8 fusion.54
  101.9 1.2 fusion.55
  103.1 0.8 copy.40
  104.0 3.2 %fusion.57 = f32[2,4,192,128]{3,2,1,0:T(8,128)} fusion(bf16[512,2,128,1]{0,2,3,1:T(8,128)(2,1)} %bitcast.53, f32[2,512,192,4]{1,2,3,0:T(8,128)S(1)} %get-tuple-element.465, f32[2,4,192]{2,1,0:T(4,128)S(1)} %ceil_maximum_fusion.2, pred[192,512]{1,0:T(8,128)(4,1)S(1)} %or_and_fusion.2, f32[2,4,192,128]{3,2,1,0:T(8,128)} %get-tuple-element.485, ...), kind=kOutput, calls=%fused_computation.9.clone.1 | convolution fusion | flops 206635008 | bytes 5091329 | tf_op jit(solution)/shard_map/while/body/eval_jaxpr/grqk,kgd->grqd/dot_general | solution.py:55
  107.2 1.4 fusion.19
  108.6 0.3 copy.28
  109.2 6.9 %fusion.35 = f32[192,4096]{1,0:T(8,128)} fusion(bf16[192,1024]{1,0:T(8,128)(2,1)S(1)} %convert_element_type.26, bf16[1024,4096]{1,0:T(8,128)(2,1)} %param.11), kind=kOutput, calls=%fused_computation.51 | convolution fusion | flops 1610612736 | bytes 11927552 | tf_op jit(solution)/shard_map/dot_general | solution.py:93
  116.1 0.6 copy-done.1
  117.0 11.5 %reduce-scatter.2.cloned.1.call-done = f32[192,2048]{1,0:T(8,128)} async-done(((f32[192,4096]{1,0:T(8,128)}), f32[192,2048]{1,0:T(8,128)}) %reduce-scatter.2.cloned.1.call-update) | async-done | bytes 1572880 | tf_op jit(solution)/shard_map/reduce_scatter | solution.py:94
  128.5 2.9 %fusion.20 = f32[16,2048]{1,0:T(8,128)} fusion(f32[192,2048]{1,0:T(8,128)} %reduce-scatter.2.cloned.1.call-done, f32[16]{0:T(128)S(1)} %get-tuple-element.393, s32[192]{0:T(256)S(1)} %iota_add_fusion.2, s32[16]{0:T(128)S(1)} %reduce.6, s32[16]{0:T(128)S(1)} %get-tuple-element.392), kind=kOutput, calls=%fused_computation.34 | convolution fusion | flops 75512832 | bytes 1704896 | tf_op jit(solution)/shard_map/dot_general | solution.py:95
  131.4 0.6 dynamic-slice
  132.6 70.4 %all-reduce.3.cloned.1.call-done = f32[16,2048]{1,0:T(8,128)} async-done(((f32[16,2048]{1,0:T(8,128)}), f32[16,2048]{1,0:T(8,128)}) %all-reduce.3.cloned.1.call-update) | async-done | bytes 131088
  203.0 1.5 constant_dynamic-slice_fusion.2
  (42 shorter events, 1.6 us)
Async XLA Ops:
  6.5 72.6 %copy-start = (s32[1,8]{1,0:T(1,128)S(1)}, s32[1,8]{1,0:T(1,128)}, u32[]{:S(2)}) copy-start(s32[1,8]{1,0:T(1,128)} %param.13) | copy-start | bytes 100
  6.5 121.9 %reduce-scatter.2.cloned.1.call-start = ((), (), s32[]{:S(2)}) async-start(), calls=%async_computation.1 | async-start | bytes 4718592 | tf_op jit(solution)/shard_map/reduce_scatter | solution.py:94
  116.1 0.7 copy-start.1
  116.1 15.3 %copy-start.2 = (u32[32]{0:T(128)S(1)}, u32[32]{0:T(128)}, u32[]{:S(2)}) copy-start(u32[32]{0:T(128)} %constant.141) | copy-start | bytes 388
  116.1 86.9 %all-reduce.3.cloned.1.call-start = ((), (), s32[]{:S(2)}) async-start(), calls=%async_computation.2 | async-start | bytes 262144
Sparse Core Ops, SparseCore 0:
  116.2 12.2 reduce-scatter.1
  132.2 70.7 all-reduce.2
where the time goes:
time: 212 us; the launch traced here: 211 us
  waiting for transfers between devices  81.9 us (39%)
  blocking collectives  70.6 us (33%)
  matrix products  24.8 us (12%)
  between operations  14.1 us (7%)
  local copies, waits for them, and re-layouts  13.6 us (6%)
  other arithmetic  6.13 us (3%)
    unnamed x3, waiting for transfers between devices  70.4 us
    all_gather x1, blocking collectives, on_device(): key_piece = lax.all_gather(key_states, 'seq', axis=0, tiled=True)  36.3 us
    all_gather x1, blocking collectives, on_device(): value_piece = lax.all_gather(value_states, 'seq', axis=0, tiled=True)  34.2 us
    reduce_scatter x1, waiting for transfers between devices, on_device(): lax.psum_scatter(partial_rows, 'head', scatter_dimension=1, tiled=True)  11.5 us
    dot_general x3, matrix products, attend(): jnp.einsum('grqk,kgd->grqd', weights.astype(jnp.bfloat16), value_rows.res...  9.53 us
    dot_general x1, matrix products, on_device(): jnp.dot(attended_work, out_weight, preferred_element_type=jnp.float32)  6.85 us
    dynamic_slice x6, local copies, waits for them, and re-layouts, one_block(): value_rows = lax.dynamic_slice_in_dim(value_piece, offset, width_step, 0)  5.76 us
    dot_general x3, matrix products, attend(): jnp.einsum('qgrd,kgd->grqk', grouped, key_rows.reshape(length, groups, HD...  5.5 us
  transfers between devices with their start and end apart: 2, of which 2 were waited for; matrix products, arithmetic and copies ran while one was open for 0% of the time, Pallas kernels for 0%

commit v1 on v0

v1 whole, which is shorter than its diff:
```python
import functools
import math

import jax
import jax.numpy as jnp
from jax import lax
from jax.experimental import pallas as pl
from jax.experimental.pallas import tpu as pltpu
from jax.sharding import PartitionSpec as P

HD = 128
CHUNK = 256
MESH = pl.DeviceIdType.MESH
big_negative = -1e30
log_two_e = 1.4426950408889634


def kernel(
    dims,
    q_hbm,
    k_hbm,
    v_hbm,
    w_hbm,
    len_ref,
    flag_ref,
    out_ref,
    kv,
    q_in,
    q_rows,
    q_turned,
    weight,
    top,
    total,
    acc,
    member,
    part,
    parts,
    lhs,
    half_out,
    half_in,
    local_sem,
    weight_sem,
    line_send,
    row_send,
    recv,
    part_send,
    part_recv,
    half_send,
    half_recv,
):
    n, inner, rows, heads, groups, turns, owned = dims
    outer = n // inner
    repeat = heads // groups
    wide = heads * rows
    factor = log_two_e / math.sqrt(HD)
    me = lax.axis_index("seq")
    head = lax.axis_index("head")
    o, i = lax.div(me, inner), lax.rem(me, inner)

    barrier = pltpu.get_barrier_semaphore()
    for j in range(1, n):
        pl.semaphore_signal(
            barrier, inc=1, device_id={"seq": lax.rem(me + j, n)}, device_id_type=MESH
        )
    pl.semaphore_signal(barrier, inc=1, device_id={"head": 1 - head}, device_id_type=MESH)

    cols = weight.shape[2]
    loads = [
        pltpu.make_async_copy(q_hbm, q_in, local_sem.at[0]),
        pltpu.make_async_copy(k_hbm, kv.at[me, 0], local_sem.at[1]),
        pltpu.make_async_copy(v_hbm, kv.at[me, 1], local_sem.at[2]),
    ]
    for load in loads:
        load.start()
    pl.semaphore_wait(barrier, n)

    def line_copy(kind, d, source):
        b = me - d * inner
        return pltpu.make_async_remote_copy(
            src_ref=source,
            dst_ref=kv.at[b, kind],
            send_sem=line_send.at[kind, d],
            recv_sem=recv.at[kind, b],
            device_id={"seq": lax.rem(me + inner, n)},
            device_id_type=MESH,
        )

    def row_copy(kind, d, j, source):
        b = me - d * inner
        return pltpu.make_async_remote_copy(
            src_ref=source,
            dst_ref=kv.at[b, kind],
            send_sem=row_send.at[kind, d, j],
            recv_sem=recv.at[kind, b],
            device_id={"seq": o * inner + lax.rem(i + j, inner)},
            device_id_type=MESH,
        )

    def sends(kind, d, source, act, own):
        @pl.when(o < outer - 1)
        def _():
            act(line_copy(kind, d, source))

        for j in range(1, inner):
            if own:

                @pl.when(lax.rem(i + j, inner) > i)
                def _():
                    act(row_copy(kind, d, j, source))

            else:
                act(row_copy(kind, d, j, source))

    def begin(copy):
        copy.start()

    def finish(copy):
        copy.wait_send()

    def arrived(kind, b):
        pltpu.make_async_copy(kv.at[b, kind], kv.at[b, kind], recv.at[kind, b]).wait()

    sends(0, 0, k_hbm, begin, True)
    sends(1, 0, v_hbm, begin, True)
    weight_loads = []
    for slot, side in ((0, 1 - head), (1, head)):
        start = pl.multiple_of(side * cols, cols)
        weight_loads.append(
            pltpu.make_async_copy(
                w_hbm.at[:, pl.ds(start, cols)], weight.at[slot], weight_sem.at[slot]
            )
        )
    for load in weight_loads:
        load.start()

    for load in loads:
        load.wait()
    for h in range(heads):
        q_rows[h * rows : (h + 1) * rows, :] = q_in[:, h * HD : (h + 1) * HD]
    q_turned[...] = q_rows[...].T

    def attend(b, diagonal):
        if not diagonal:
            seen = jnp.full((1, CHUNK), flag_ref[0, b], jnp.int32) == 1
        for g in range(groups):
            keys = kv[b, 0, :, g * HD : (g + 1) * HD]
            values = kv[b, 1, :, g * HD : (g + 1) * HD].T
            for c in range(g * repeat * rows, (g + 1) * repeat * rows, CHUNK):
                here = slice(c, c + CHUNK)
                logit = jnp.dot(keys, q_turned[:, here], preferred_element_type=jnp.float32)
                if diagonal:
                    column = c + lax.broadcasted_iota(jnp.int32, (1, CHUNK), 1)
                    token = column
                    for h in range(1, heads):
                        token = jnp.where(column >= h * rows, column - h * rows, token)
                    key = lax.broadcasted_iota(jnp.int32, (rows, CHUNK), 0)
                    logit = jnp.where(key <= token, logit, big_negative)
                    new_top = jnp.ceil(jnp.max(logit, axis=0, keepdims=True) * factor)
                    shift = new_top
                else:
                    old_top = top[:, here]
                    block_top = jnp.ceil(jnp.max(logit, axis=0, keepdims=True) * factor)
                    new_top = jnp.maximum(old_top, jnp.where(seen, block_top, big_negative))
                    shift = jnp.where(seen, new_top, -big_negative)
                weights = jnp.exp2(logit * factor - shift)
                added = jnp.sum(weights, axis=0, keepdims=True)
                update = jnp.dot(
                    values, weights.astype(jnp.bfloat16), preferred_element_type=jnp.float32
                )
                top[:, here] = new_top
                if diagonal:
                    total[:, here] = added
                    acc[:, here] = update
                else:
                    rescale = jnp.exp2(old_top - new_top)
                    total[:, here] = total[:, here] * rescale + added
                    acc[:, here] = acc[:, here] * rescale + update

    attend(me, True)

    lengths = len_ref[...].astype(jnp.float32)
    row = lax.broadcasted_iota(jnp.int32, (turns * heads, turns), 0)
    turn_of_row = lax.div(row, heads)
    head_of_row = (row - turn_of_row * heads)[:, :1].astype(jnp.float32)
    turn = lax.broadcasted_iota(jnp.int32, (turns * heads, turns), 1)
    spread = jnp.broadcast_to(lengths, (turns * heads, turns))
    starts = jnp.sum(jnp.where(turn < turn_of_row, spread, 0.0), axis=1, keepdims=True)
    length = jnp.sum(jnp.where(turn == turn_of_row, spread, 0.0), axis=1, keepdims=True)
    base = (me * rows).astype(jnp.float32)
    low = head_of_row * rows + jnp.clip(starts - base, 0.0, rows)
    high = head_of_row * rows + jnp.clip(starts + length - base, 0.0, rows)
    column = lax.broadcasted_iota(jnp.int32, (turns * heads, wide), 1).astype(jnp.float32)
    member[...] = jnp.where((column >= low) & (column < high), 1.0, 0.0).astype(jnp.bfloat16)
    share = 1.0 / length

    def row_blocks(d, own):
        for j in range(1, inner):
            place = lax.rem(i + j, inner)
            b = (o - d) * inner + place

            def take():
                arrived(0, b)
                arrived(1, b)
                attend(b, False)

            if own:
                pl.when(place < i)(take)
            else:
                take()

    row_blocks(0, True)

    def step(d, carry):
        b = me - d * inner
        arrived(0, b)
        sends(0, d, kv.at[b, 0], begin, False)
        arrived(1, b)
        sends(1, d, kv.at[b, 1], begin, False)
        attend(b, False)
        row_blocks(d, False)
        return carry

    lax.fori_loop(1, o + 1, step, 0)

    attended = (acc[...] * (1.0 / total[...])).astype(jnp.bfloat16)
    pooled = lax.dot_general(
        member[...],
        attended,
        (((1,), (1,)), ((), ())),
        preferred_element_type=jnp.float32,
    )
    part[...] = (pooled * share).reshape(turns, heads, HD)

    def part_copy(j):
        peer = lax.rem(me + j, n)
        return pltpu.make_async_remote_copy(
            src_ref=part.at[pl.ds(peer * owned, owned)],
            dst_ref=parts.at[me],
            send_sem=part_send.at[j],
            recv_sem=part_recv.at[me],
            device_id={"seq": peer},
            device_id_type=MESH,
        )

    for j in range(1, n):
        part_copy(j).start()
    mine = part[pl.ds(me * owned, owned)]

    def gather(j, summed):
        peer = lax.rem(me + j, n)
        pltpu.make_async_copy(parts.at[peer], parts.at[peer], part_recv.at[peer]).wait()
        return summed + parts[peer]

    summed = lax.fori_loop(1, n, gather, mine)
    flat = jnp.concatenate([summed[:, h, :] for h in range(heads)], axis=1)
    high_part = flat.astype(jnp.bfloat16).astype(jnp.float32)
    rest = flat - high_part
    middle_part = rest.astype(jnp.bfloat16).astype(jnp.float32)
    lhs[...] = jnp.zeros_like(lhs)
    lhs[0:owned, :] = high_part
    lhs[owned : 2 * owned, :] = middle_part
    lhs[2 * owned : 3 * owned, :] = rest - middle_part
    operand = lhs[...].astype(jnp.bfloat16)

    def project(slot):
        weight_loads[slot].wait()
        wide_out = jnp.dot(operand, weight[slot], preferred_element_type=jnp.float32)
        return (
            wide_out[0:owned] + wide_out[owned : 2 * owned] + wide_out[2 * owned : 3 * owned]
        )

    half_out[...] = project(0)
    half = pltpu.make_async_remote_copy(
        src_ref=half_out,
        dst_ref=half_in,
        send_sem=half_send,
        recv_sem=half_recv,
        device_id={"head": 1 - head},
        device_id_type=MESH,
    )
    half.start()
    own_half = project(1)

    sends(0, 0, k_hbm, finish, True)
    sends(1, 0, v_hbm, finish, True)

    def settle(d, carry):
        b = me - d * inner
        sends(0, d, kv.at[b, 0], finish, False)
        sends(1, d, kv.at[b, 1], finish, False)
        return carry

    lax.fori_loop(1, o + 1, settle, 0)
    for j in range(1, n):
        part_copy(j).wait_send()
    half.wait()
    out_ref[...] = own_half + half_in[...]


def on_device(n, nh, queries, key_states, value_states, out_weight, turn_lengths, block_flags):
    rows = queries.shape[0]
    heads = queries.shape[1] // HD
    groups = key_states.shape[1] // HD
    turns = turn_lengths.shape[0]
    owned = turns // n
    depth, width = out_weight.shape
    cols = width // nh
    inner = 2 if n <= 8 else 8
    outer = n // inner
    wide = heads * rows
    dims = (n, inner, rows, heads, groups, turns, owned)
    lhs_rows = -(-3 * owned // 8) * 8
    dma = pltpu.SemaphoreType.DMA
    any_spec = pl.BlockSpec(memory_space=pl.ANY)
    return pl.pallas_call(
        functools.partial(kernel, dims),
        out_shape=jax.ShapeDtypeStruct((owned, cols), jnp.float32),
        in_specs=[any_spec] * 4
        + [
            pl.BlockSpec(memory_space=pltpu.VMEM),
            pl.BlockSpec(memory_space=pltpu.SMEM),
        ],
        out_specs=pl.BlockSpec(memory_space=pltpu.VMEM),
        scratch_shapes=[
            pltpu.VMEM((n, 2, rows, groups * HD), jnp.bfloat16),
            pltpu.VMEM((rows, heads * HD), jnp.bfloat16),
            pltpu.VMEM((wide, HD), jnp.bfloat16),
            pltpu.VMEM((HD, wide), jnp.bfloat16),
            pltpu.VMEM((nh, depth, cols), jnp.bfloat16),
            pltpu.VMEM((1, wide), jnp.float32),
            pltpu.VMEM((1, wide), jnp.float32),
            pltpu.VMEM((HD, wide), jnp.float32),
            pltpu.VMEM((turns * heads, wide), jnp.bfloat16),
            pltpu.VMEM((turns, heads, HD), jnp.float32),
            pltpu.VMEM((n, owned, heads, HD), jnp.float32),
            pltpu.VMEM((lhs_rows, depth), jnp.float32),
            pltpu.VMEM((owned, cols), jnp.float32),
            pltpu.VMEM((owned, cols), jnp.float32),
            dma((3,)),
            dma((2,)),
            dma((2, outer)),
            dma((2, outer, inner)),
            dma((2, n)),
            dma((n,)),
            dma((n,)),
            dma,
            dma,
        ],
        compiler_params=pltpu.CompilerParams(
            collective_id=0, has_side_effects=True, vmem_limit_bytes=56 << 20
        ),
    )(
        queries,
        key_states,
        value_states,
        out_weight,
        turn_lengths.reshape(1, turns),
        block_flags,
    )


def solution(mesh):
    in_specs = (
        P(("conv", "seq"), "head"),
        P(("conv", "seq"), "head"),
        P(("conv", "seq"), "head"),
        P("head", None),
        P("conv"),
        P(("conv", "seq"), None),
    )
    out_specs = P(("conv", "seq"), "head")
    return jax.shard_map(
        functools.partial(on_device, mesh.shape["seq"], mesh.shape["head"]),
        mesh=mesh,
        in_specs=in_specs,
        out_specs=out_specs,
        check_vma=False,
    )
```

time: 212 us -> 43.7 us (0.21)
  waiting for transfers between devices: 81.9 us -> 0 us
  blocking collectives: 70.6 us -> 0 us
  Pallas kernels: 0 us -> 42.2 us
  matrix products: 24.8 us -> 0 us
  between operations: 14.1 us -> 0.01 us
  local copies, waits for them, and re-layouts: 13.6 us -> 1.32 us
  other arithmetic: 6.13 us -> 0 us
    all_gather x2 -> x0, blocking collectives: 70.6 us -> none  [the longest x1 36.3 us: on_device(): key_piece = lax.all_gather(key_states, 'seq', axis=0, tiled=True)]
    unnamed x3 -> x0, waiting for transfers between devices: 70.4 us -> none
    pallas_call x0 -> x1, Pallas kernels: none -> 42.2 us  [on_device(): pl.pallas_call(functools.partial(kernel, dims), out_shape=jax.ShapeDtypeS...]
    dot_general x8 -> x0, matrix products: 24.8 us -> none  [the longest x3 9.53 us: attend(): jnp.einsum('grqk,kgd->grqd', weights.astype(jnp.bfloat16), value_rows.res...]
    reduce_scatter x1 -> x0, waiting for transfers between devices: 11.5 us -> none  [on_device(): lax.psum_scatter(partial_rows, 'head', scatter_dimension=1, tiled=True)]
    dynamic_slice x9 -> x0, local copies, waits for them, and re-layouts: 8.3 us -> none  [the longest x6 5.76 us: one_block(): value_rows = lax.dynamic_slice_in_dim(value_piece, offset, width_step, 0)]
    reduce_sum x6 -> x0, other arithmetic: 3.85 us -> none  [the longest x3 3.59 us: attend(): run_sum = run_sum * rescale + jnp.sum(weights, axis=-1)]
  transfers between devices with their start and end apart: 2 -> 0, of which waited for: 2 -> 0; matrix products, arithmetic and copies ran while one was open for 0% -> 0% of each run, Pallas kernels for 0% -> 0%
where the time goes in v1:
time: 43.7 us; the launch traced here: 43.5 us
  Pallas kernels  42.2 us (97%)
  local copies, waits for them, and re-layouts  1.32 us (3%)
    pallas_call x1, Pallas kernels, on_device(): pl.pallas_call(functools.partial(kernel, dims), out_shape=jax.ShapeDtypeS...  42.2 us
    unnamed x1, local copies, waits for them, and re-layouts  1.32 us

profile of v1, /device:TPU:0, one launch (start us, length us, event | category | flops | bytes accessed | tf_op | source)
XLA Modules:
  0.0 43.5 jit_solution(5914253934971027830)
XLA Ops:
  0.0 42.2 %shard_map.64 = f32[2,2048]{1,0:T(2,128)} custom-call(bf16[192,1024]{1,0:T(8,128)(2,1)} %q_hbm.1, bf16[192,256]{1,0:T(8,128)(2,1)} %k_hbm.1, bf16[192,256]{1,0:T(8,128)(2,1)} %v_hbm.1, bf16[1024,4096]{1,0:T(8,128)(2,1)} %w_hbm.1, s32[1,16]{1,0:T(1,128)} %bitcast.1, s32[1,8]{1,0:T(1,128)} %flag_ref.1), custom_call_target="tpu_custom_call" | custom-call | tf_op jit(solution)/shard_map/pallas_call | solution.py:315
  42.2 1.3 %copy.8 = f32[2,2048]{1,0:T(2,128)} copy(f32[2,2048]{1,0:T(2,128)} %shard_map.64) | data formatting | bytes 32768

commit v2 on v1

--- a/solution.py
+++ b/solution.py
@@ -36,17 +36,14 @@
     part,
     parts,
     lhs,
-    half_out,
-    half_in,
     local_sem,
     weight_sem,
     line_send,
     row_send,
     recv,
+    side_send,
     part_send,
     part_recv,
-    half_send,
-    half_recv,
 ):
     n, inner, rows, heads, groups, turns, owned = dims
     outer = n // inner
@@ -58,11 +55,12 @@
     o, i = lax.div(me, inner), lax.rem(me, inner)
 
     barrier = pltpu.get_barrier_semaphore()
-    for j in range(1, n):
-        pl.semaphore_signal(
-            barrier, inc=1, device_id={"seq": lax.rem(me + j, n)}, device_id_type=MESH
-        )
-    pl.semaphore_signal(barrier, inc=1, device_id={"head": 1 - head}, device_id_type=MESH)
+    for j in range(n):
+        peer = lax.rem(me + j, n)
+        for core in (1 - head, head) if j else (1 - head,):
+            pl.semaphore_signal(
+                barrier, inc=1, device_id={"seq": peer, "head": core}, device_id_type=MESH
+            )
 
     cols = weight.shape[2]
     loads = [
@@ -72,7 +70,7 @@
     ]
     for load in loads:
         load.start()
-    pl.semaphore_wait(barrier, n)
+    pl.semaphore_wait(barrier, 2 * n - 1)
 
     def line_copy(kind, d, source):
         b = me - d * inner
@@ -108,9 +106,26 @@
                 def _():
                     act(row_copy(kind, d, j, source))
 
+            elif kind == 1 and inner == 2:
+
+                @pl.when((i == 1) | (d > 1))
+                def _():
+                    act(row_copy(kind, d, j, source))
+
             else:
                 act(row_copy(kind, d, j, source))
 
+    def side_copy():
+        b = o * inner
+        return pltpu.make_async_remote_copy(
+            src_ref=kv.at[b, 1],
+            dst_ref=kv.at[b, 1],
+            send_sem=side_send,
+            recv_sem=recv.at[1, b],
+            device_id={"seq": lax.rem(me + inner, n)},
+            device_id_type=MESH,
+        )
+
     def begin(copy):
         copy.start()
 
@@ -122,16 +137,21 @@
 
     sends(0, 0, k_hbm, begin, True)
     sends(1, 0, v_hbm, begin, True)
-    weight_loads = []
-    for slot, side in ((0, 1 - head), (1, head)):
-        start = pl.multiple_of(side * cols, cols)
-        weight_loads.append(
-            pltpu.make_async_copy(
-                w_hbm.at[:, pl.ds(start, cols)], weight.at[slot], weight_sem.at[slot]
-            )
-        )
-    for load in weight_loads:
-        load.start()
+    start = pl.multiple_of(head * cols, cols)
+    other = pl.multiple_of((1 - head) * cols, cols)
+    weight_load = pltpu.make_async_copy(
+        w_hbm.at[:, pl.ds(start, cols)], weight.at[0], weight_sem.at[0]
+    )
+    weight_swap = pltpu.make_async_remote_copy(
+        src_ref=w_hbm.at[:, pl.ds(other, cols)],
+        dst_ref=weight.at[1],
+        send_sem=weight_sem.at[1],
+        recv_sem=weight_sem.at[2],
+        device_id={"head": 1 - head},
+        device_id_type=MESH,
+    )
+    weight_load.start()
+    weight_swap.start()
 
     for load in loads:
         load.wait()
@@ -193,22 +213,30 @@
     member[...] = jnp.where((column >= low) & (column < high), 1.0, 0.0).astype(jnp.bfloat16)
     share = 1.0 / length
 
-    def row_blocks(d, own):
+    def row_blocks(d):
         for j in range(1, inner):
             place = lax.rem(i + j, inner)
             b = (o - d) * inner + place
 
-            def take():
-                arrived(0, b)
-                arrived(1, b)
+            @pl.when((place < i) | (d > 0))
+            def _():
+                @pl.when((d > 0) | (inner != 2))
+                def _():
+                    arrived(0, b)
+                    arrived(1, b)
+
                 attend(b, False)
 
-            if own:
-                pl.when(place < i)(take)
-            else:
-                take()
-
-    row_blocks(0, True)
+    if inner == 2:
+
+        @pl.when(i == 1)
+        def _():
+            arrived(0, me - 1)
+            arrived(1, me - 1)
+
+            @pl.when(o < outer - 1)
+            def _():
+                side_copy().start()
 
     def step(d, carry):
         b = me - d * inner
@@ -216,11 +244,12 @@
         sends(0, d, kv.at[b, 0], begin, False)
         arrived(1, b)
         sends(1, d, kv.at[b, 1], begin, False)
+        row_blocks(d - 1)
         attend(b, False)
-        row_blocks(d, False)
         return carry
 
     lax.fori_loop(1, o + 1, step, 0)
+    row_blocks(o)
 
     attended = (acc[...] * (1.0 / total[...])).astype(jnp.bfloat16)
     pooled = lax.dot_general(
@@ -231,58 +260,57 @@
     )
     part[...] = (pooled * share).reshape(turns, heads, HD)
 
-    def part_copy(j):
+    def part_copy(away, j):
         peer = lax.rem(me + j, n)
         return pltpu.make_async_remote_copy(
             src_ref=part.at[pl.ds(peer * owned, owned)],
-            dst_ref=parts.at[me],
-            send_sem=part_send.at[j],
-            recv_sem=part_recv.at[me],
-            device_id={"seq": peer},
+            dst_ref=parts.at[head, me],
+            send_sem=part_send.at[away, j],
+            recv_sem=part_recv.at[head, me],
+            device_id={"seq": peer, "head": 1 - head if away else head},
             device_id_type=MESH,
         )
 
-    for j in range(1, n):
-        part_copy(j).start()
-    mine = part[pl.ds(me * owned, owned)]
-
-    def gather(j, summed):
+    pairs = [(away, j) for j in range(n) for away in (0, 1) if away or j]
+    for away, j in pairs:
+        part_copy(away, j).start()
+
+    def gather(away, j):
         peer = lax.rem(me + j, n)
-        pltpu.make_async_copy(parts.at[peer], parts.at[peer], part_recv.at[peer]).wait()
-        return summed + parts[peer]
-
-    summed = lax.fori_loop(1, n, gather, mine)
-    flat = jnp.concatenate([summed[:, h, :] for h in range(heads)], axis=1)
-    high_part = flat.astype(jnp.bfloat16).astype(jnp.float32)
-    rest = flat - high_part
-    middle_part = rest.astype(jnp.bfloat16).astype(jnp.float32)
+        core = 1 - head if away else head
+        here = parts.at[core, peer]
+        pltpu.make_async_copy(here, here, part_recv.at[core, peer]).wait()
+        return parts[core, peer]
+
+    sums = [part[pl.ds(me * owned, owned)], None]
+    for away, j in pairs:
+        piece = gather(away, j)
+        sums[away] = piece if sums[away] is None else sums[away] + piece
+
     lhs[...] = jnp.zeros_like(lhs)
-    lhs[0:owned, :] = high_part
-    lhs[owned : 2 * owned, :] = middle_part
-    lhs[2 * owned : 3 * owned, :] = rest - middle_part
-    operand = lhs[...].astype(jnp.bfloat16)
-
-    def project(slot):
-        weight_loads[slot].wait()
-        wide_out = jnp.dot(operand, weight[slot], preferred_element_type=jnp.float32)
-        return (
-            wide_out[0:owned] + wide_out[owned : 2 * owned] + wide_out[2 * owned : 3 * owned]
-        )
-
-    half_out[...] = project(0)
-    half = pltpu.make_async_remote_copy(
-        src_ref=half_out,
-        dst_ref=half_in,
-        send_sem=half_send,
-        recv_sem=half_recv,
-        device_id={"head": 1 - head},
-        device_id_type=MESH,
-    )
-    half.start()
-    own_half = project(1)
+    for slot, summed in enumerate(sums):
+        flat = jnp.concatenate([summed[:, h, :] for h in range(heads)], axis=1)
+        high_part = flat.astype(jnp.bfloat16).astype(jnp.float32)
+        rest = flat - high_part
+        middle_part = rest.astype(jnp.bfloat16).astype(jnp.float32)
+        lhs[slot, 0:owned, :] = high_part
+        lhs[slot, owned : 2 * owned, :] = middle_part
+        lhs[slot, 2 * owned : 3 * owned, :] = rest - middle_part
+
+    weight_load.wait()
+    weight_swap.wait()
+    result = jnp.dot(
+        lhs[0].astype(jnp.bfloat16), weight[0], preferred_element_type=jnp.float32
+    ) + jnp.dot(lhs[1].astype(jnp.bfloat16), weight[1], preferred_element_type=jnp.float32)
+    out_ref[...] = result[0:owned] + result[owned : 2 * owned] + result[2 * owned : 3 * owned]
 
     sends(0, 0, k_hbm, finish, True)
     sends(1, 0, v_hbm, finish, True)
+    if inner == 2:
+
+        @pl.when((i == 1) & (o < outer - 1))
+        def _():
+            side_copy().wait_send()
 
     def settle(d, carry):
         b = me - d * inner
@@ -291,10 +319,8 @@
         return carry
 
     lax.fori_loop(1, o + 1, settle, 0)
-    for j in range(1, n):
-        part_copy(j).wait_send()
-    half.wait()
-    out_ref[...] = own_half + half_in[...]
+    for away, j in pairs:
+        part_copy(away, j).wait_send()
 
 
 def on_device(n, nh, queries, key_states, value_states, out_weight, turn_lengths, block_flags):
@@ -332,19 +358,16 @@
             pltpu.VMEM((HD, wide), jnp.float32),
             pltpu.VMEM((turns * heads, wide), jnp.bfloat16),
             pltpu.VMEM((turns, heads, HD), jnp.float32),
-            pltpu.VMEM((n, owned, heads, HD), jnp.float32),
-            pltpu.VMEM((lhs_rows, depth), jnp.float32),
-            pltpu.VMEM((owned, cols), jnp.float32),
-            pltpu.VMEM((owned, cols), jnp.float32),
+            pltpu.VMEM((nh, n, owned, heads, HD), jnp.float32),
+            pltpu.VMEM((nh, lhs_rows, depth), jnp.float32),
             dma((3,)),
-            dma((2,)),
+            dma((3,)),
             dma((2, outer)),
             dma((2, outer, inner)),
             dma((2, n)),
-            dma((n,)),
-            dma((n,)),
             dma,
-            dma,
+            dma((nh, n)),
+            dma((nh, n)),
         ],
         compiler_params=pltpu.CompilerParams(
             collective_id=0, has_side_effects=True, vmem_limit_bytes=56 << 20

time: 43.7 us -> 40.1 us (0.918)
  Pallas kernels: 42.2 us -> 38.6 us
    pallas_call x1, Pallas kernels: 42.2 us -> 38.6 us  [on_device(): pl.pallas_call(functools.partial(kernel, dims), out_shape=jax.ShapeDtypeS...]
where the time goes in v2:
time: 40.1 us; the launch traced here: 39.9 us
  Pallas kernels  38.6 us (96%)
  local copies, waits for them, and re-layouts  1.32 us (3%)
    pallas_call x1, Pallas kernels, on_device(): pl.pallas_call(functools.partial(kernel, dims), out_shape=jax.ShapeDtypeS...  38.6 us
    unnamed x1, local copies, waits for them, and re-layouts  1.32 us

profile of v2, /device:TPU:0, one launch (start us, length us, event | category | flops | bytes accessed | tf_op | source)
XLA Modules:
  0.0 39.9 jit_solution(15276851824648266225)
XLA Ops:
  0.0 38.6 %shard_map.64 = f32[2,2048]{1,0:T(2,128)} custom-call(bf16[192,1024]{1,0:T(8,128)(2,1)} %q_hbm.1, bf16[192,256]{1,0:T(8,128)(2,1)} %k_hbm.1, bf16[192,256]{1,0:T(8,128)(2,1)} %v_hbm.1, bf16[1024,4096]{1,0:T(8,128)(2,1)} %w_hbm.1, s32[1,16]{1,0:T(1,128)} %bitcast.1, s32[1,8]{1,0:T(1,128)} %flag_ref.1), custom_call_target="tpu_custom_call" | custom-call | tf_op jit(solution)/shard_map/pallas_call | solution.py:341
  38.6 1.3 %copy.8 = f32[2,2048]{1,0:T(2,128)} copy(f32[2,2048]{1,0:T(2,128)} %shard_map.64) | data formatting | bytes 32768

commit v3 on v2

--- a/solution.py
+++ b/solution.py
@@ -41,11 +41,10 @@
     line_send,
     row_send,
     recv,
-    side_send,
     part_send,
     part_recv,
 ):
-    n, inner, rows, heads, groups, turns, owned = dims
+    n, inner, rows, heads, groups, turns, owned, pieces = dims
     outer = n // inner
     repeat = heads // groups
     wide = heads * rows
@@ -65,9 +64,16 @@
     cols = weight.shape[2]
     loads = [
         pltpu.make_async_copy(q_hbm, q_in, local_sem.at[0]),
-        pltpu.make_async_copy(k_hbm, kv.at[me, 0], local_sem.at[1]),
-        pltpu.make_async_copy(v_hbm, kv.at[me, 1], local_sem.at[2]),
     ]
+    short = rows // pieces
+
+    def own_piece(kind):
+        return (k_hbm, v_hbm)[kind // pieces].at[pl.ds(kind % pieces * short, short)]
+
+    for kind in range(2 * pieces):
+        loads.append(
+            pltpu.make_async_copy(own_piece(kind), kv.at[me, kind], local_sem.at[1 + kind])
+        )
     for load in loads:
         load.start()
     pl.semaphore_wait(barrier, 2 * n - 1)
@@ -106,26 +112,9 @@
                 def _():
                     act(row_copy(kind, d, j, source))
 
-            elif kind == 1 and inner == 2:
-
-                @pl.when((i == 1) | (d > 1))
-                def _():
-                    act(row_copy(kind, d, j, source))
-
             else:
                 act(row_copy(kind, d, j, source))
 
-    def side_copy():
-        b = o * inner
-        return pltpu.make_async_remote_copy(
-            src_ref=kv.at[b, 1],
-            dst_ref=kv.at[b, 1],
-            send_sem=side_send,
-            recv_sem=recv.at[1, b],
-            device_id={"seq": lax.rem(me + inner, n)},
-            device_id_type=MESH,
-        )
-
     def begin(copy):
         copy.start()
 
@@ -135,8 +124,8 @@
     def arrived(kind, b):
         pltpu.make_async_copy(kv.at[b, kind], kv.at[b, kind], recv.at[kind, b]).wait()
 
-    sends(0, 0, k_hbm, begin, True)
-    sends(1, 0, v_hbm, begin, True)
+    for kind in range(2 * pieces):
+        sends(kind, 0, own_piece(kind), begin, True)
     start = pl.multiple_of(head * cols, cols)
     other = pl.multiple_of((1 - head) * cols, cols)
     weight_load = pltpu.make_async_copy(
@@ -163,8 +152,9 @@
         if not diagonal:
             seen = jnp.full((1, CHUNK), flag_ref[0, b], jnp.int32) == 1
         for g in range(groups):
-            keys = kv[b, 0, :, g * HD : (g + 1) * HD]
-            values = kv[b, 1, :, g * HD : (g + 1) * HD].T
+            lanes = slice(g * HD, (g + 1) * HD)
+            keys = kv[b, :pieces, :, lanes].reshape(rows, HD)
+            values = kv[b, pieces:, :, lanes].reshape(rows, HD).T
             for c in range(g * repeat * rows, (g + 1) * repeat * rows, CHUNK):
                 here = slice(c, c + CHUNK)
                 logit = jnp.dot(keys, q_turned[:, here], preferred_element_type=jnp.float32)
@@ -220,30 +210,15 @@
 
             @pl.when((place < i) | (d > 0))
             def _():
-                @pl.when((d > 0) | (inner != 2))
-                def _():
-                    arrived(0, b)
-                    arrived(1, b)
-
+                for kind in range(2 * pieces):
+                    arrived(kind, b)
                 attend(b, False)
-
-    if inner == 2:
-
-        @pl.when(i == 1)
-        def _():
-            arrived(0, me - 1)
-            arrived(1, me - 1)
-
-            @pl.when(o < outer - 1)
-            def _():
-                side_copy().start()
 
     def step(d, carry):
         b = me - d * inner
-        arrived(0, b)
-        sends(0, d, kv.at[b, 0], begin, False)
-        arrived(1, b)
-        sends(1, d, kv.at[b, 1], begin, False)
+        for kind in range(2 * pieces):
+            arrived(kind, b)
+            sends(kind, d, kv.at[b, kind], begin, False)
         row_blocks(d - 1)
         attend(b, False)
         return carry
@@ -304,18 +279,12 @@
     ) + jnp.dot(lhs[1].astype(jnp.bfloat16), weight[1], preferred_element_type=jnp.float32)
     out_ref[...] = result[0:owned] + result[owned : 2 * owned] + result[2 * owned : 3 * owned]
 
-    sends(0, 0, k_hbm, finish, True)
-    sends(1, 0, v_hbm, finish, True)
-    if inner == 2:
-
-        @pl.when((i == 1) & (o < outer - 1))
-        def _():
-            side_copy().wait_send()
-
+    for kind in range(2 * pieces):
+        sends(kind, 0, own_piece(kind), finish, True)
     def settle(d, carry):
         b = me - d * inner
-        sends(0, d, kv.at[b, 0], finish, False)
-        sends(1, d, kv.at[b, 1], finish, False)
+        for kind in range(2 * pieces):
+            sends(kind, d, kv.at[b, kind], finish, False)
         return carry
 
     lax.fori_loop(1, o + 1, settle, 0)
@@ -334,7 +303,8 @@
     inner = 2 if n <= 8 else 8
     outer = n // inner
     wide = heads * rows
-    dims = (n, inner, rows, heads, groups, turns, owned)
+    pieces = 2 if rows % 32 == 0 else 1
+    dims = (n, inner, rows, heads, groups, turns, owned, pieces)
     lhs_rows = -(-3 * owned // 8) * 8
     dma = pltpu.SemaphoreType.DMA
     any_spec = pl.BlockSpec(memory_space=pl.ANY)
@@ -348,7 +318,7 @@
         ],
         out_specs=pl.BlockSpec(memory_space=pltpu.VMEM),
         scratch_shapes=[
-            pltpu.VMEM((n, 2, rows, groups * HD), jnp.bfloat16),
+            pltpu.VMEM((n, 2 * pieces, rows // pieces, groups * HD), jnp.bfloat16),
             pltpu.VMEM((rows, heads * HD), jnp.bfloat16),
             pltpu.VMEM((wide, HD), jnp.bfloat16),
             pltpu.VMEM((HD, wide), jnp.bfloat16),
@@ -360,12 +330,11 @@
             pltpu.VMEM((turns, heads, HD), jnp.float32),
             pltpu.VMEM((nh, n, owned, heads, HD), jnp.float32),
             pltpu.VMEM((nh, lhs_rows, depth), jnp.float32),
+            dma((1 + 2 * pieces,)),
             dma((3,)),
-            dma((3,)),
-            dma((2, outer)),
-            dma((2, outer, inner)),
-            dma((2, n)),
-            dma,
+            dma((2 * pieces, outer)),
+            dma((2 * pieces, outer, inner)),
+            dma((2 * pieces, n)),
             dma((nh, n)),
             dma((nh, n)),
         ],

time: 40.1 us -> 37.2 us (0.928)
  Pallas kernels: 38.6 us -> 35.6 us
    pallas_call x1, Pallas kernels: 38.6 us -> 35.6 us  [on_device(): pl.pallas_call(functools.partial(kernel, dims), out_shape=jax.ShapeDtypeS...]
where the time goes in v3:
time: 37.2 us; the launch traced here: 37 us
  Pallas kernels  35.6 us (96%)
  local copies, waits for them, and re-layouts  1.32 us (4%)
    pallas_call x1, Pallas kernels, on_device(): pl.pallas_call(functools.partial(kernel, dims), out_shape=jax.ShapeDtypeS...  35.6 us
    unnamed x1, local copies, waits for them, and re-layouts  1.32 us

profile of v3, /device:TPU:0, one launch (start us, length us, event | category | flops | bytes accessed | tf_op | source)
XLA Modules:
  0.0 37.0 jit_solution(991297470309555128)
XLA Ops:
  0.0 35.6 %shard_map.64 = f32[2,2048]{1,0:T(2,128)} custom-call(bf16[192,1024]{1,0:T(8,128)(2,1)} %q_hbm.1, bf16[192,256]{1,0:T(8,128)(2,1)} %k_hbm.1, bf16[192,256]{1,0:T(8,128)(2,1)} %v_hbm.1, bf16[1024,4096]{1,0:T(8,128)(2,1)} %w_hbm.1, s32[1,16]{1,0:T(1,128)} %bitcast.1, s32[1,8]{1,0:T(1,128)} %flag_ref.1), custom_call_target="tpu_custom_call" | custom-call | tf_op jit(solution)/shard_map/pallas_call | solution.py:311
  35.6 1.3 %copy.8 = f32[2,2048]{1,0:T(2,128)} copy(f32[2,2048]{1,0:T(2,128)} %shard_map.64) | data formatting | bytes 32768

commit v4 on v3

--- a/solution.py
+++ b/solution.py
@@ -219,8 +219,8 @@
         for kind in range(2 * pieces):
             arrived(kind, b)
             sends(kind, d, kv.at[b, kind], begin, False)
+        attend(b, False)
         row_blocks(d - 1)
-        attend(b, False)
         return carry
 
     lax.fori_loop(1, o + 1, step, 0)

time: 37.2 us -> 37.2 us (level)
  no operation moved by 1% of the time
where the time goes in v4:
time: 37.2 us; the launch traced here: 37 us
  Pallas kernels  35.6 us (96%)
  local copies, waits for them, and re-layouts  1.32 us (4%)
    pallas_call x1, Pallas kernels, on_device(): pl.pallas_call(functools.partial(kernel, dims), out_shape=jax.ShapeDtypeS...  35.6 us
    unnamed x1, local copies, waits for them, and re-layouts  1.32 us

profile of v4, /device:TPU:0, one launch (start us, length us, event | category | flops | bytes accessed | tf_op | source)
XLA Modules:
  0.0 37.0 jit_solution(12868100286271380804)
XLA Ops:
  0.0 35.6 %shard_map.64 = f32[2,2048]{1,0:T(2,128)} custom-call(bf16[192,1024]{1,0:T(8,128)(2,1)} %q_hbm.1, bf16[192,256]{1,0:T(8,128)(2,1)} %k_hbm.1, bf16[192,256]{1,0:T(8,128)(2,1)} %v_hbm.1, bf16[1024,4096]{1,0:T(8,128)(2,1)} %w_hbm.1, s32[1,16]{1,0:T(1,128)} %bitcast.1, s32[1,8]{1,0:T(1,128)} %flag_ref.1), custom_call_target="tpu_custom_call" | custom-call | tf_op jit(solution)/shard_map/pallas_call | solution.py:311
  35.6 1.3 %copy.8 = f32[2,2048]{1,0:T(2,128)} copy(f32[2,2048]{1,0:T(2,128)} %shard_map.64) | data formatting | bytes 32768
